TPU v7x, 32 devices: a whole 2x2x4 slice. The times are simulated.
32 devices in a mesh: angle: 8 (over z, y), tile: 2 (over x), half: 2 (over core).
Axes of the slice: x: 2, y: 2, z: 4, core: 2. Of those that a mesh axis runs over, the one named last changes fastest.
Arguments:
- projection: float32 [16, 2, 64, 256], P(('angle', 'half'), None, 'tile'), may hold values from -6 to 6
- multiplier: float32 [16, 2, 64, 256], P(('angle', 'half'), None, 'tile'), may hold values from -3 to 3
- reprojection: float32 [16, 64, 256], P(('angle', 'half'), 'tile'), may hold values from -6 to 6
- intensity: bfloat16 [16, 64, 64, 128], P(('angle', 'half'), 'tile'), may hold values from 0 to 4
- row_start: int32 [16, 64], P(('angle', 'half'), 'tile'), may hold values from -32 to 0
- column_start: int32 [16, 64], P(('angle', 'half'), 'tile'), may hold values from 0 to 128
- probe_field: float32 [2, 64, 128], replicated, may hold values from -6 to 6
- probe_mask: int32 [64, 128], replicated, may hold values 0 or 1
- weights: bfloat16 [16, 2, 4, 128, 512], P('angle'), may hold values from -0.125 to 0.125
- ray_blocks: int32 [16, 2, 4], P('angle'), may hold values from 0 to 127, as said below
- ray_counts: int32 [16, 2], P('angle'), may hold values from 1 to 4, as said below
- volume: float32 [128, 64, 512], P('angle', ('tile', 'half')), may hold values from -6 to 6
Outputs:
- updated_projection: float32 [16, 2, 64, 256], P(('angle', 'half'), None, 'tile')
- volume_new: float32 [128, 64, 512], P('angle', ('tile', 'half'))
- multiplier_new: float32 [16, 2, 64, 256], P('angle', None, ('tile', 'half'))
Inputs may be any that keep to these rules, and one draw needn't show every extreme that they name: A ray block uses its first ray_counts weight tiles; some ray block uses all 4. `ray_blocks`: slots at or past a ray block's count are not used. Split the angles into aligned groups of 2 and the pixel blocks into aligned groups of 16: the 16 slots of one angle group name blocks of one block group at most 2 times, and exactly 2 times for some block group.
All inputs are finite; a program needn't handle non-finite values.
Results may differ from a plain program's by a relative error of at most 0.008.
Values may be sent and summed in bfloat16 or wider, within the bound.
A program may use at most 64 MiB of HBM per device.

v0:
```python
import functools

import jax
import jax.numpy as jnp
import numpy as np
from jax import lax
from jax.experimental import pallas as pl
from jax.experimental.pallas import tpu as pltpu
from jax.sharding import PartitionSpec as P

PR = 64
PC = 128
NW = 256
PIX = 512
RB = 128
CMAX = 4
HALO = 32
NRB = 2


penalty = 0.5
descent = 0.25
volume_step = 1.0
damping = 0.1


def dft_blocks(sign):
    def table(length):
        counter = np.arange(length)
        phase = (counter[:, None] * counter[None, :] % length) * (2.0 * np.pi / length)
        return np.cos(phase) / np.sqrt(length), sign * np.sin(phase) / np.sqrt(length)

    row_cos, row_sin = table(PR)
    col_cos, col_sin = table(PC)
    left = np.block([[row_cos, -row_sin], [row_sin, row_cos]])
    right = np.block([[col_cos, col_sin], [-col_sin, col_cos]])
    return left.astype(np.float32), right.astype(np.float32)


def split_table(matrix):
    coarse = matrix.astype(jnp.bfloat16)
    rest = (matrix - coarse.astype(np.float32)).astype(jnp.bfloat16)
    return jnp.asarray(np.concatenate([coarse, rest], axis=1))


MESH = pl.DeviceIdType.MESH
CHUNK = 16


def step_kernel(
    groups, tiles, capacity,
    mine_ref, counts_ref, rows_ref, cols_ref,
    ids_ref, proj_ref, mult_ref, prior_ref, measured_ref, field_ref, mask_ref,
    left_f_ref, right_f_ref, left_b_ref, right_b_ref, vol_ref, weight_hbm,
    updated_ref, new_vol_ref, new_mult_ref,
    all_ref, all_smem, wanted_ref, place_ref, slot_ref, used_ref, live_ref,
    weight_ref, before_ref, after_ref, above_ref, below_ref,
    ext_ref, acc_ref, wave_ref, stage_ref,
    moved_ref, mult_moved_ref, half_send_ref,
    send_a, send_b, send_c, recv_a, recv_b, recv_c, spread_ref, wide_ref,
    send_sem, recv_sem, near_send, near_recv, local_sem,
):
    g = lax.axis_index("angle")
    t = lax.axis_index("tile")
    h = lax.axis_index("half")
    band = proj_ref.shape[2]
    part = band // 2
    places = groups * capacity
    own_blocks = vol_ref.shape[0]
    angles, blocks, per_block = mine_ref.shape
    slots = angles * blocks * per_block
    has_up = t > 0
    has_down = t < tiles - 1
    half = jnp.bfloat16
    sends = (send_a, send_b, send_c)
    recvs = (recv_a, recv_b, recv_c)
    lanes = [slice(0, PC), slice(PC, NW)]

    def where_of(slot):
        pair, c = divmod(slot, per_block)
        angle, block = divmod(pair, blocks)
        return angle, block, c

    barrier = pltpu.get_barrier_semaphore()

    def greet(where):
        pl.semaphore_signal(barrier, inc=1, device_id=where, device_id_type=MESH)

    for d in range(1, groups):
        greet({"angle": lax.rem(g + d, groups)})
    greet({"half": 1 - h})

    @pl.when(has_up)
    def _():
        greet({"tile": t - 1})

    @pl.when(has_down)
    def _():
        greet({"tile": t + 1})

    weight_copy = pltpu.make_async_copy(weight_hbm, weight_ref, local_sem.at[0])
    weight_copy.start()

    owners = [lax.div(mine_ref[where_of(s)], own_blocks) for s in range(slots)]
    my_places = []
    for s in range(slots):
        rank = jnp.int32(0)
        for earlier in range(s):
            rank = rank + jnp.where(owners[earlier] == owners[s], 1, 0)
        my_places.append(owners[s] * capacity + rank)
        place_ref[s] = my_places[s]
        angle, block, c = where_of(s)
        live_ref[s] = jnp.where(c < counts_ref[angle, block], 1.0, 0.0)

    def slot_of(n, carry):
        slot = jnp.int32(0)
        used = jnp.float32(0.0)
        for s in range(slots):
            hit = place_ref[s] == n
            slot = jnp.where(hit, s, slot)
            used = jnp.where(hit, 1.0, used)
        slot_ref[n] = slot
        used_ref[n] = used
        return carry

    pl.semaphore_wait(barrier, groups + has_up.astype(jnp.int32) + has_down.astype(jnp.int32))

    def angle_copy(phase, d, source, target):
        return pltpu.make_async_remote_copy(
            src_ref=source,
            dst_ref=target,
            send_sem=send_sem.at[phase, d],
            recv_sem=recv_sem.at[phase, d],
            device_id={"angle": lax.rem(g + d, groups)},
            device_id_type=MESH,
        )

    id_copies = [angle_copy(3, d, ids_ref, all_ref.at[g]) for d in range(1, groups)]
    for copy in id_copies:
        copy.start()

    def exchange(phase):
        copies = []
        for d in range(1, groups):
            peer = lax.rem(g + d, groups)
            copies.append(
                angle_copy(
                    phase, d,
                    sends[phase].at[pl.ds(peer * capacity, capacity)],
                    recvs[phase].at[pl.ds(g * capacity, capacity)],
                )
            )
            copies[-1].start()
        own = pl.ds(g * capacity, capacity)
        recvs[phase][own] = sends[phase][own]
        return copies

    def near(index, source, target, where):
        return pltpu.make_async_remote_copy(
            src_ref=source,
            dst_ref=target,
            send_sem=near_send.at[index],
            recv_sem=near_recv.at[index],
            device_id=where,
            device_id_type=MESH,
        )

    def to_tiles(index, down_source, down_target, up_source, up_target):
        down = near(index, down_source, down_target, {"tile": jnp.minimum(t + 1, tiles - 1)})
        up = near(index + 1, up_source, up_target, {"tile": jnp.maximum(t - 1, 0)})

        @pl.when(has_down)
        def _():
            down.start()

        @pl.when(has_up)
        def _():
            up.start()

        @pl.when(jnp.logical_not(has_up))
        def _():
            down_target[...] = jnp.zeros_like(down_target)

        @pl.when(jnp.logical_not(has_down))
        def _():
            up_target[...] = jnp.zeros_like(up_target)

        return down, up

    def from_tiles(down, up):
        @pl.when(has_up)
        def _():
            down.wait_recv()

        @pl.when(has_down)
        def _():
            up.wait_recv()

    def sent_to_tiles(down, up):
        @pl.when(has_down)
        def _():
            down.wait_send()

        @pl.when(has_up)
        def _():
            up.wait_send()

    halo = to_tiles(
        0, proj_ref.at[0, :, band - HALO :, :], before_ref, proj_ref.at[0, :, :HALO, :], after_ref
    )
    away = pl.ds(pl.multiple_of((1 - h) * part, part), part)
    here = pl.ds(pl.multiple_of(h * part, part), part)
    mult_copy = near(4, mult_ref.at[0, :, away, :], mult_moved_ref.at[h], {"half": 1 - h})
    mult_copy.start()
    mult_moved_ref[h] = mult_ref[0, :, here, :]
    all_ref[g] = ids_ref[...]
    lax.fori_loop(0, places, slot_of, 0)
    for side in range(2):
        ext_ref[:, side, HALO : HALO + band] = proj_ref[0, :, :, lanes[side]]
    acc_ref[...] = jnp.zeros_like(acc_ref)
    stage_ref[...] = jnp.zeros_like(stage_ref)
    mask = mask_ref[...].astype(jnp.float32)
    wave_ref[0] = field_ref[0] * mask
    wave_ref[1] = field_ref[1] * mask

    for copy in id_copies:
        copy.wait_recv()
    id_local = pltpu.make_async_copy(all_ref, all_smem, local_sem.at[1])
    id_local.start()
    id_local.wait()

    def group(peer, carry):
        found = jnp.int32(0)
        values = [jnp.int32(0)] * capacity
        for s in range(slots):
            b = all_smem[(peer,) + where_of(s)]
            hit = lax.div(b, own_blocks) == g
            inside = lax.rem(b, own_blocks)
            values = [
                jnp.where(jnp.logical_and(hit, found == r), inside, values[r])
                for r in range(capacity)
            ]
            found = found + jnp.where(hit, 1, 0)
        for r in range(capacity):
            wanted_ref[peer * capacity + r] = values[r]
        return carry

    lax.fori_loop(0, groups, group, 0)
    for n in range(places):
        send_a[n] = vol_ref[wanted_ref[n]].astype(half)
    fetches = exchange(0)
    from_tiles(*halo)
    for side in range(2):
        ext_ref[:, side, :HALO] = before_ref[:, :, lanes[side]]
        ext_ref[:, side, HALO + band :] = after_ref[:, :, lanes[side]]

    lane = lax.broadcasted_iota(jnp.int32, (PR, PC), 1)
    ext_rows = band + 2 * HALO
    wide_lane = lax.broadcasted_iota(jnp.int32, (ext_rows, PC), 1)

    def dot(a, b):
        return jnp.dot(a, b, preferred_element_type=jnp.float32)

    def step(chunk, carry):
        waves = []
        spots = []
        for j in range(CHUNK):
            p = chunk * CHUNK + j
            row = rows_ref[0, p] + HALO
            col = cols_ref[0, p]
            spots.append((row, col))
            back_shift = lax.rem(NW - col, PC)

            def window(channel):
                near = pltpu.roll(ext_ref[channel, 0, pl.ds(row, PR), :], back_shift, 1)
                next_ = pltpu.roll(ext_ref[channel, 1, pl.ds(row, PR), :], back_shift, 1)
                return jnp.where(lane + col < PC, near, next_)

            o_re = window(0)
            o_im = window(1)
            p_re, p_im = wave_ref[0], wave_ref[1]
            waves.append(
                jnp.concatenate([p_re * o_re - p_im * o_im, p_re * o_im + p_im * o_re], axis=0)
            )
        wide = jnp.concatenate(waves, axis=1).astype(half)
        first = dot(left_f_ref[...], jnp.concatenate([wide, wide], axis=0)).astype(half)
        tall = jnp.concatenate(
            [
                jnp.concatenate(
                    [first[:PR, j * PC : (j + 1) * PC], first[PR:, j * PC : (j + 1) * PC]], axis=1
                )
                for j in range(CHUNK)
            ],
            axis=0,
        )
        far = dot(tall, right_f_ref[...])
        f_re, f_im = far[:, :PC], far[:, PC:]
        measured = measured_ref[0, pl.ds(chunk * CHUNK, CHUNK)].astype(jnp.float32)
        measured = measured.reshape(CHUNK * PR, PC)
        factor = 1.0 - jnp.sqrt(measured) * lax.rsqrt(f_re * f_re + f_im * f_im + 1.0)
        scaled = jnp.concatenate([f_re * factor, f_im * factor], axis=1).astype(half)
        second = dot(scaled, right_b_ref[...]).astype(half)
        wide = jnp.concatenate(
            [
                jnp.concatenate(
                    [second[j * PR : (j + 1) * PR, :PC], second[j * PR : (j + 1) * PR, PC:]], axis=0
                )
                for j in range(CHUNK)
            ],
            axis=1,
        )
        back = dot(left_b_ref[...], jnp.concatenate([wide, wide], axis=0))
        above = ext_rows - PR
        for j in range(CHUNK):
            shift = lax.rem(spots[j][1], PC)
            b_re = back[:PR, j * PC : (j + 1) * PC]
            b_im = back[PR:, j * PC : (j + 1) * PC]
            p_re, p_im = wave_ref[0], wave_ref[1]
            stage_ref[j, 0, above : above + PR] = pltpu.roll(p_re * b_re + p_im * b_im, shift, 1)
            stage_ref[j, 1, above : above + PR] = pltpu.roll(p_re * b_im - p_im * b_re, shift, 1)
        for channel in range(2):
            first_half = acc_ref[channel, 0]
            next_half = acc_ref[channel, 1]
            for j in range(CHUNK):
                row, col = spots[j]
                values = stage_ref[j, channel, pl.ds(above - row, ext_rows), :]
                first_half = first_half + jnp.where(wide_lane >= col, values, 0.0)
                next_half = next_half + jnp.where(wide_lane >= col, 0.0, values)
            acc_ref[channel, 0] = first_half
            acc_ref[channel, 1] = next_half
        return carry

    lax.fori_loop(0, rows_ref.shape[1] // CHUNK, step, 0)
    rims = to_tiles(
        2, acc_ref.at[:, :, HALO + band :, :], above_ref, acc_ref.at[:, :, :HALO, :], below_ref
    )
    from_tiles(*rims)
    for side in range(2):
        for channel in range(2):
            gradient = acc_ref[channel, side, HALO : HALO + band]
            above = above_ref[channel, side]
            below = below_ref[channel, side]
            if band == HALO:
                gradient = gradient + above + below
            else:
                still = jnp.zeros((band - HALO, PC), jnp.float32)
                gradient = gradient + jnp.concatenate([above, still], axis=0)
                gradient = gradient + jnp.concatenate([still, below], axis=0)
            old = proj_ref[0, channel, :, lanes[side]]
            held = 1.0 if channel == 0 else prior_ref[0, :, lanes[side]]
            updated_ref[0, channel, :, lanes[side]] = old - descent * (
                gradient + penalty * (old - held) + mult_ref[0, channel, :, lanes[side]]
            )
    half_send_ref[...] = updated_ref[0, :, away, :]
    moved_copy = near(5, half_send_ref, moved_ref.at[h], {"half": 1 - h})
    moved_copy.start()
    moved_ref[h] = updated_ref[0, :, here, :]
    for copy in fetches:
        copy.wait_recv()
    mult_copy.wait_recv()
    weight_copy.wait()

    def projected(phase, pair):
        total = jnp.zeros((part, RB), jnp.float32)
        for c in range(per_block):
            slot = pair * per_block + c
            picked = recvs[phase][place_ref[slot]]
            total = total + live_ref[slot] * lax.dot_general(
                picked, weight_ref[where_of(slot)], (((1,), (1,)), ((), ())),
                preferred_element_type=jnp.float32,
            )
        return total

    pairs = slots // per_block
    sinos = [projected(0, pair) for pair in range(pairs)]
    moved_copy.wait_recv()
    for pair in range(pairs):
        angle, k = divmod(pair, NRB)
        rays = slice(k * RB, (k + 1) * RB)
        target = moved_ref[angle, 1, :, rays] + mult_moved_ref[angle, 1, :, rays] / penalty
        residual = (sinos[pair] - target).astype(half)
        for c in range(per_block):
            slot = pair * per_block + c
            spread = live_ref[slot] * jnp.dot(
                residual, weight_ref[where_of(slot)], preferred_element_type=jnp.float32
            )
            spread_ref[slot] = spread.astype(half)
    for n in range(places):
        send_b[n] = spread_ref[slot_ref[n]] * used_ref[n].astype(half)
    terms = exchange(1)
    for copy in terms:
        copy.wait_recv()
    for n in range(places):
        wide_ref[n] = recv_b[n].astype(jnp.float32)

    def renew(j, carry):
        total = jnp.zeros(wide_ref.shape[1:], jnp.float32)
        for n in range(places):
            total = total + jnp.where(wanted_ref[n] == j, 1.0, 0.0) * wide_ref[n]
        block = vol_ref[j]
        new_vol_ref[j] = block - volume_step * (total + damping * block)
        return carry

    lax.fori_loop(0, own_blocks, renew, 0)
    for n in range(places):
        send_c[n] = new_vol_ref[wanted_ref[n]].astype(half)
    renewals = exchange(2)
    for angle in range(moved_ref.shape[0]):
        new_mult_ref[angle, 0] = mult_moved_ref[angle, 0] + penalty * (moved_ref[angle, 0] - 1.0)
    for copy in renewals:
        copy.wait_recv()
    for pair in range(pairs):
        angle, k = divmod(pair, NRB)
        rays = slice(k * RB, (k + 1) * RB)
        fresh = projected(2, pair)
        new_mult_ref[angle, 1, :, rays] = mult_moved_ref[angle, 1, :, rays] + penalty * (
            moved_ref[angle, 1, :, rays] - fresh
        )
    for copy in id_copies + fetches + terms + renewals + [mult_copy, moved_copy]:
        copy.wait_send()
    sent_to_tiles(*halo)
    sent_to_tiles(*rims)


def admm_step(ray_blocks, counts, rows, cols, own, multiplier, prior, measured, field, mask, volume, weights):
    groups = lax.axis_size("angle")
    tiles = lax.axis_size("tile")
    slots = ray_blocks.size
    capacity = max(2, -(-slots // groups))
    places = groups * capacity
    left_f, right_f = dft_blocks(-1.0)
    left_b, right_b = dft_blocks(1.0)
    left_f, left_b = (split_table(m) for m in (left_f, left_b))
    tables = [left_f, jnp.asarray(right_f, jnp.bfloat16), left_b, jnp.asarray(right_b, jnp.bfloat16)]
    vmem = pl.BlockSpec(memory_space=pltpu.VMEM)
    smem = pl.BlockSpec(memory_space=pltpu.SMEM)
    band = own.shape[2]
    ext_rows = band + 2 * HALO
    block = volume.shape[1:]
    moved_shape = (2, 2, band // 2, NW)
    ids = (groups,) + ray_blocks.shape
    f32 = jnp.float32
    return pl.pallas_call(
        functools.partial(step_kernel, groups, tiles, capacity),
        out_shape=(
            jax.ShapeDtypeStruct(own.shape, f32),
            jax.ShapeDtypeStruct(volume.shape, f32),
            jax.ShapeDtypeStruct(moved_shape, f32),
        ),
        in_specs=[smem] * 4 + [vmem] * 12 + [pl.BlockSpec(memory_space=pl.ANY)],
        out_specs=(vmem, vmem, vmem),
        scratch_shapes=[
            pltpu.VMEM(ids, jnp.int32),
            pltpu.SMEM(ids, jnp.int32),
            pltpu.SMEM((places,), jnp.int32),
            pltpu.SMEM((slots,), jnp.int32),
            pltpu.SMEM((places,), jnp.int32),
            pltpu.SMEM((places,), f32),
            pltpu.SMEM((slots,), f32),
            pltpu.VMEM(weights.shape, jnp.bfloat16),
            pltpu.VMEM((2, HALO, NW), f32),
            pltpu.VMEM((2, HALO, NW), f32),
            pltpu.VMEM((2, NW // PC, HALO, PC), f32),
            pltpu.VMEM((2, NW // PC, HALO, PC), f32),
            pltpu.VMEM((2, NW // PC, ext_rows, PC), f32),
            pltpu.VMEM((2, NW // PC, ext_rows, PC), f32),
            pltpu.VMEM((2, PR, PC), f32),
            pltpu.VMEM((CHUNK, 2, 2 * (ext_rows - PR) + PR, PC), f32),
            pltpu.VMEM(moved_shape, f32),
            pltpu.VMEM(moved_shape, f32),
            pltpu.VMEM(moved_shape[1:], f32),
            *[pltpu.VMEM((places,) + block, jnp.bfloat16)] * 6,
            pltpu.VMEM((slots,) + block, jnp.bfloat16),
            pltpu.VMEM((places,) + block, f32),
            pltpu.SemaphoreType.DMA((4, groups)),
            pltpu.SemaphoreType.DMA((4, groups)),
            pltpu.SemaphoreType.DMA((6,)),
            pltpu.SemaphoreType.DMA((6,)),
            pltpu.SemaphoreType.DMA((2,)),
        ],
        compiler_params=pltpu.CompilerParams(collective_id=1, has_side_effects=True),
    )(
        ray_blocks, counts, rows, cols,
        ray_blocks, own, multiplier, prior, measured, field, mask, *tables, volume, weights,
    )


def write_kernel(a_ref, b_ref, c_ref, a_out, b_out, c_out, sems):
    copies = [
        pltpu.make_async_copy(source, target, sems.at[i])
        for i, (source, target) in enumerate(((a_ref, a_out), (b_ref, b_out), (c_ref, c_out)))
    ]
    for copy in copies:
        copy.start()
    for copy in copies:
        copy.wait()


def write_out(values):
    return pl.pallas_call(
        write_kernel,
        out_shape=tuple(jax.ShapeDtypeStruct(v.shape, v.dtype) for v in values),
        in_specs=[pl.BlockSpec(memory_space=pltpu.VMEM)] * 3,
        out_specs=tuple([pl.BlockSpec(memory_space=pl.ANY)] * 3),
        scratch_shapes=[pltpu.SemaphoreType.DMA((3,))],
    )(*values)


def shards(
    projection,
    multiplier,
    reprojection,
    intensity,
    row_start,
    column_start,
    probe_field,
    probe_mask,
    weights,
    ray_blocks,
    ray_counts,
    volume,
):
    return write_out(
        admm_step(
            ray_blocks, ray_counts, row_start, column_start, projection, multiplier, reprojection,
            intensity, probe_field, probe_mask, volume, weights,
        )
    )


def solution(mesh):
    return jax.shard_map(
        shards,
        mesh=mesh,
        in_specs=(
            P(("angle", "half"), None, "tile", None),
            P(("angle", "half"), None, "tile", None),
            P(("angle", "half"), "tile", None),
            P(("angle", "half"), "tile", None, None),
            P(("angle", "half"), "tile"),
            P(("angle", "half"), "tile"),
            P(),
            P(),
            P("angle", None, None, None, None),
            P("angle", None, None),
            P("angle", None),
            P("angle", ("tile", "half"), None),
        ),
        out_specs=(
            P(("angle", "half"), None, "tile", None),
            P("angle", ("tile", "half"), None),
            P("angle", None, ("tile", "half"), None),
        ),
        check_vma=False,
    )
```

profile of v0, /device:TPU:0, one launch (start us, length us, event | category | flops | bytes accessed | tf_op | source)
XLA Modules:
  0.0 40.1 jit_solution(2346384347163550304)
XLA Ops:
  0.6 37.6 %shard_map.175 = (f32[1,2,32,256]{3,2,1,0:T(8,128)}, f32[16,16,512]{2,1,0:T(8,128)}, f32[2,2,16,256]{3,2,1,0:T(8,128)}) custom-call(s32[2,2,4]{2,1,0:T(2,128)} %ids_ref.1, s32[2,2]{1,0:T(2,128)} %counts_ref.1, s32[1,32]{1,0:T(1,128)} %rows_ref.1, s32[1,32]{1,0:T(1,128)} %cols_ref.1, s32[2,2,4]{2,1,0:T(2,128)} %ids_ref.1, f32[1,2,32,256]{3,2,1,0:T(8,128)} %proj_ref.1, ...), custom_call_target="tpu_custom_call" | custom-call | tf_op jit(solution)/shard_map/pallas_call | solution.py:443
  38.3 1.9 %shard_map.176 = (f32[1,2,32,256]{3,2,1,0:T(8,128)}, f32[16,16,512]{2,1,0:T(8,128)}, f32[2,2,16,256]{3,2,1,0:T(8,128)}) custom-call(f32[1,2,32,256]{3,2,1,0:T(8,128)} %get-tuple-element.6.a_ref, f32[16,16,512]{2,1,0:T(8,128)} %get-tuple-element.7.b_ref, f32[2,2,16,256]{3,2,1,0:T(8,128)} %get-tuple-element.8.c_ref), custom_call_target="tpu_custom_call" | custom-call | tf_op jit(solution)/shard_map/pallas_call | solution.py:500
where the time goes:
time: 40.3 us; the launch traced here: 40.1 us
  Pallas kernels  39.5 us (98%)
  between operations  0.64 us (2%)
    pallas_call x1, Pallas kernels, admm_step(): pl.pallas_call(functools.partial(step_kernel, groups, tiles, capacity), o...  37.6 us
    pallas_call x1, Pallas kernels, write_out(): pl.pallas_call(write_kernel, out_shape=tuple((jax.ShapeDtypeStruct(v.shap...  1.89 us

commit v1 on v0

v1 whole, which is shorter than its diff:
```python
import functools

import jax
import jax.numpy as jnp
import numpy as np
from jax import lax
from jax.experimental import pallas as pl
from jax.experimental.pallas import tpu as pltpu
from jax.sharding import PartitionSpec as P

PR = 64
PC = 128
NW = 256
PIX = 512
RB = 128
CMAX = 4
HALO = 32
NRB = 2


penalty = 0.5
descent = 0.25
volume_step = 1.0
damping = 0.1


def dft_blocks(sign):
    def table(length):
        counter = np.arange(length)
        phase = (counter[:, None] * counter[None, :] % length) * (2.0 * np.pi / length)
        return np.cos(phase) / np.sqrt(length), sign * np.sin(phase) / np.sqrt(length)

    row_cos, row_sin = table(PR)
    col_cos, col_sin = table(PC)
    left = np.block([[row_cos, -row_sin], [row_sin, row_cos]])
    right = np.block([[col_cos, col_sin], [-col_sin, col_cos]])
    return left.astype(np.float32), right.astype(np.float32)


def split_table(matrix):
    coarse = matrix.astype(jnp.bfloat16)
    rest = (matrix - coarse.astype(np.float32)).astype(jnp.bfloat16)
    return jnp.asarray(np.concatenate([coarse, rest], axis=1))


MESH = pl.DeviceIdType.MESH
CHUNK = 16
ROWS = 8
LANES = 128


def orders(groups):
    rising = list(range(1, groups))
    paired = []
    for d in range(1, groups // 2 + 1):
        paired += [groups - d] if 2 * d == groups else [groups - d, d]
    if groups % 2:
        paired = rising
    return rising, paired


def step_kernel(
    groups, tiles, capacity,
    mine_hbm, counts_hbm, rows_hbm, cols_hbm, proj_hbm, mult_hbm, prior_hbm, field_hbm, mask_hbm,
    left_f_hbm, right_f_hbm, left_b_hbm, right_b_hbm, measured_hbm, vol_hbm, weight_hbm,
    updated_ref, new_vol_ref, new_mult_ref,
    mine_ref, counts_ref, rows_ref, cols_ref, proj_ref, mult_ref, prior_ref, field_ref, mask_ref,
    left_f_ref, right_f_ref, left_b_ref, right_b_ref, measured_ref, vol_ref, weight_ref,
    all_smem, place_ref, inside_ref, slot_ref, used_ref, live_ref,
    ids_ref, all_ref, edge_ref, before_ref, after_ref,
    ext_ref, acc_ref, wave_ref, stage_ref,
    base_ref, grad_ref, both_base_ref, both_mult_ref, both_grad_ref,
    rim_ref, rim_here_ref, rim_away_ref,
    vol_half_ref, merge_ref, residual_ref,
    send_a, send_b, send_c, recv_a, recv_b, recv_c,
    send_sem, recv_sem, near_send, near_recv, local_sem,
):
    g = lax.axis_index("angle")
    t = lax.axis_index("tile")
    h = lax.axis_index("half")
    band = proj_ref.shape[2]
    part = band // 2
    places = groups * capacity
    own_blocks = vol_ref.shape[0]
    angles, blocks, per_block = mine_ref.shape
    slots = angles * blocks * per_block
    pairs = slots // per_block
    has_up = t > 0
    has_down = t < tiles - 1
    half = jnp.bfloat16
    sends = (send_a, send_b, send_c)
    recvs = (recv_a, recv_b, recv_c)
    lanes = [slice(0, PC), slice(PC, NW)]
    rising, paired = orders(groups)

    def where_of(slot):
        pair, c = divmod(slot, per_block)
        angle, block = divmod(pair, blocks)
        return angle, block, c

    barrier = pltpu.get_barrier_semaphore()

    def greet(where):
        pl.semaphore_signal(barrier, inc=1, device_id=where, device_id_type=MESH)

    for d in rising:
        greet({"angle": lax.rem(g + d, groups)})
    greet({"half": 1 - h})

    @pl.when(has_up)
    def _():
        greet({"tile": t - 1})
        greet({"tile": t - 1, "half": 1 - h})

    @pl.when(has_down)
    def _():
        greet({"tile": t + 1})
        greet({"tile": t + 1, "half": 1 - h})

    sources = (
        mine_hbm, counts_hbm, rows_hbm, cols_hbm, proj_hbm, mult_hbm, prior_hbm, field_hbm, mask_hbm,
        left_f_hbm, right_f_hbm, left_b_hbm, right_b_hbm, measured_hbm, vol_hbm, weight_hbm,
    )
    targets = (
        mine_ref, counts_ref, rows_ref, cols_ref, proj_ref, mult_ref, prior_ref, field_ref, mask_ref,
        left_f_ref, right_f_ref, left_b_ref, right_b_ref, measured_ref, vol_ref, weight_ref,
    )
    loads = [
        pltpu.make_async_copy(source, target, local_sem.at[i])
        for i, (source, target) in enumerate(zip(sources, targets))
    ]
    for load in loads:
        load.start()

    @pl.when(jnp.logical_not(has_up))
    def _():
        before_ref[...] = jnp.zeros_like(before_ref)
        rim_here_ref[0] = jnp.zeros(rim_here_ref.shape[1:], half)
        rim_away_ref[0] = jnp.zeros(rim_away_ref.shape[1:], half)

    @pl.when(jnp.logical_not(has_down))
    def _():
        after_ref[...] = jnp.zeros_like(after_ref)
        rim_here_ref[1] = jnp.zeros(rim_here_ref.shape[1:], half)
        rim_away_ref[1] = jnp.zeros(rim_away_ref.shape[1:], half)

    acc_ref[...] = jnp.zeros_like(acc_ref)
    stage_ref[...] = jnp.zeros_like(stage_ref)
    ids_ref[...] = jnp.zeros_like(ids_ref)

    for load in loads[:2]:
        load.wait()
    blocks_of = [mine_ref[where_of(s)] for s in range(slots)]
    owners = [lax.div(b, own_blocks) for b in blocks_of]
    for s in range(slots):
        rank = jnp.int32(0)
        for earlier in range(s):
            rank = rank + jnp.where(owners[earlier] == owners[s], 1, 0)
        place_ref[s] = owners[s] * capacity + rank
        inside_ref[s] = lax.rem(blocks_of[s], own_blocks)
        angle, block, c = where_of(s)
        live_ref[s] = jnp.where(c < counts_ref[angle, block], 1.0, 0.0)

    def slot_of(n, carry):
        slot = jnp.int32(0)
        used = jnp.float32(0.0)
        for s in range(slots):
            hit = place_ref[s] == n
            slot = jnp.where(hit, s, slot)
            used = jnp.where(hit, live_ref[s], used)
        slot_ref[n] = slot
        used_ref[n] = used
        return carry

    lax.fori_loop(0, places, slot_of, 0)
    for n in range(places):
        q, r = divmod(n, capacity)
        ids_ref[q, r : r + 1, :] = jnp.full((1, LANES), inside_ref[slot_ref[n]], jnp.int32)

    away = pl.ds(pl.multiple_of((1 - h) * part, part), part)
    here = pl.ds(pl.multiple_of(h * part, part), part)
    for load in loads[4:9]:
        load.wait()
    edge_ref[...] = proj_ref[0].astype(half)
    for channel in range(2):
        old = proj_ref[0, channel]
        held = 1.0 if channel == 0 else prior_ref[0]
        base_ref[channel] = old - descent * (penalty * (old - held) + mult_ref[0, channel])
    for side in range(2):
        ext_ref[:, side, HALO : HALO + band] = proj_ref[0, :, :, lanes[side]]
    mask = mask_ref[...].astype(jnp.float32)
    wave_ref[0] = field_ref[0] * mask
    wave_ref[1] = field_ref[1] * mask
    both_base_ref[h] = base_ref[:, here, :]
    both_mult_ref[h] = mult_ref[0, :, here, :]
    loads[14].wait()
    vol_half_ref[...] = vol_ref[...].astype(half)

    pl.semaphore_wait(
        barrier, groups + 2 * has_up.astype(jnp.int32) + 2 * has_down.astype(jnp.int32)
    )

    def angle_copy(phase, d, source, target):
        return pltpu.make_async_remote_copy(
            src_ref=source,
            dst_ref=target,
            send_sem=send_sem.at[phase, d],
            recv_sem=recv_sem.at[phase, d],
            device_id={"angle": lax.rem(g + d, groups)},
            device_id_type=MESH,
        )

    def near(index, source, target, where):
        return pltpu.make_async_remote_copy(
            src_ref=source,
            dst_ref=target,
            send_sem=near_send.at[index],
            recv_sem=near_recv.at[index],
            device_id=where,
            device_id_type=MESH,
        )

    below = jnp.minimum(t + 1, tiles - 1)
    upper = jnp.maximum(t - 1, 0)

    def when_sent(way, act):
        pl.when(has_down if way == 0 else has_up)(act)

    def when_received(way, act):
        pl.when(has_up if way == 0 else has_down)(act)

    id_copies = [
        angle_copy(3, d, ids_ref.at[lax.rem(g + d, groups)], all_ref.at[g]) for d in rising
    ]
    for copy in id_copies:
        copy.start()
    halo = [
        near(0, edge_ref, before_ref, {"tile": below}),
        near(1, edge_ref, after_ref, {"tile": upper}),
    ]
    for way in range(2):
        when_sent(way, halo[way].start)
    base_copy = near(2, base_ref.at[:, away, :], both_base_ref.at[h], {"half": 1 - h})
    mult_copy = near(3, mult_ref.at[0, :, away, :], both_mult_ref.at[h], {"half": 1 - h})
    base_copy.start()
    mult_copy.start()
    all_ref[g] = ids_ref[g]
    for load in loads[2:4] + loads[9:14]:
        load.wait()
    for way in range(2):
        when_received(way, halo[way].wait_recv)
    for side in range(2):
        ext_ref[:, side, :HALO] = before_ref[:, :, lanes[side]].astype(jnp.float32)
        ext_ref[:, side, HALO + band :] = after_ref[:, :, lanes[side]].astype(jnp.float32)

    lane = lax.broadcasted_iota(jnp.int32, (PR, PC), 1)
    ext_rows = band + 2 * HALO
    wide_lane = lax.broadcasted_iota(jnp.int32, (ext_rows, PC), 1)

    def dot(a, b):
        return jnp.dot(a, b, preferred_element_type=jnp.float32)

    def step(chunk, carry):
        waves = []
        spots = []
        for j in range(CHUNK):
            p = chunk * CHUNK + j
            row = rows_ref[0, p] + HALO
            col = cols_ref[0, p]
            spots.append((row, col))
            back_shift = lax.rem(NW - col, PC)

            def window(channel):
                near = pltpu.roll(ext_ref[channel, 0, pl.ds(row, PR), :], back_shift, 1)
                next_ = pltpu.roll(ext_ref[channel, 1, pl.ds(row, PR), :], back_shift, 1)
                return jnp.where(lane + col < PC, near, next_)

            o_re = window(0)
            o_im = window(1)
            p_re, p_im = wave_ref[0], wave_ref[1]
            waves.append(
                jnp.concatenate([p_re * o_re - p_im * o_im, p_re * o_im + p_im * o_re], axis=0)
            )
        wide = jnp.concatenate(waves, axis=1).astype(half)
        first = dot(left_f_ref[...], jnp.concatenate([wide, wide], axis=0)).astype(half)
        tall = jnp.concatenate(
            [
                jnp.concatenate(
                    [first[:PR, j * PC : (j + 1) * PC], first[PR:, j * PC : (j + 1) * PC]], axis=1
                )
                for j in range(CHUNK)
            ],
            axis=0,
        )
        far = dot(tall, right_f_ref[...])
        f_re, f_im = far[:, :PC], far[:, PC:]
        measured = measured_ref[0, pl.ds(chunk * CHUNK, CHUNK)].astype(jnp.float32)
        measured = measured.reshape(CHUNK * PR, PC)
        factor = 1.0 - jnp.sqrt(measured) * lax.rsqrt(f_re * f_re + f_im * f_im + 1.0)
        scaled = jnp.concatenate([f_re * factor, f_im * factor], axis=1).astype(half)
        second = dot(scaled, right_b_ref[...]).astype(half)
        wide = jnp.concatenate(
            [
                jnp.concatenate(
                    [second[j * PR : (j + 1) * PR, :PC], second[j * PR : (j + 1) * PR, PC:]], axis=0
                )
                for j in range(CHUNK)
            ],
            axis=1,
        )
        back = dot(left_b_ref[...], jnp.concatenate([wide, wide], axis=0))
        above = ext_rows - PR
        for j in range(CHUNK):
            shift = lax.rem(spots[j][1], PC)
            b_re = back[:PR, j * PC : (j + 1) * PC]
            b_im = back[PR:, j * PC : (j + 1) * PC]
            p_re, p_im = wave_ref[0], wave_ref[1]
            stage_ref[j, 0, above : above + PR] = pltpu.roll(p_re * b_re + p_im * b_im, shift, 1)
            stage_ref[j, 1, above : above + PR] = pltpu.roll(p_re * b_im - p_im * b_re, shift, 1)
        for channel in range(2):
            first_half = acc_ref[channel, 0]
            next_half = acc_ref[channel, 1]
            for j in range(CHUNK):
                row, col = spots[j]
                values = stage_ref[j, channel, pl.ds(above - row, ext_rows), :]
                first_half = first_half + jnp.where(wide_lane >= col, values, 0.0)
                next_half = next_half + jnp.where(wide_lane >= col, 0.0, values)
            acc_ref[channel, 0] = first_half
            acc_ref[channel, 1] = next_half
        return carry

    lax.fori_loop(0, 1, step, 0)

    for copy in id_copies:
        copy.wait_recv()
    id_local = pltpu.make_async_copy(all_ref, all_smem, local_sem.at[len(loads)])
    id_local.start()
    reach = own_blocks * part
    skew = lax.broadcasted_iota(jnp.int32, (part, reach), 1) - lax.broadcasted_iota(
        jnp.int32, (part, reach), 0
    )
    picks = []
    for n in range(places):
        q, r = divmod(n, capacity)
        want = jnp.concatenate([all_ref[q, r : r + 1, :]] * (reach // LANES), axis=1)
        picks.append(jnp.where(skew == want * part, 1.0, 0.0).astype(half))
    gathered = dot(jnp.concatenate(picks, axis=0), vol_half_ref[...].reshape(reach, PIX)).astype(half)
    for n in range(places):
        send_a[n] = gathered[n * part : (n + 1) * part]

    def exchange_copy(phase, d):
        peer = lax.rem(g + d, groups)
        return angle_copy(
            phase, d,
            sends[phase].at[pl.ds(peer * capacity, capacity)],
            recvs[phase].at[pl.ds(g * capacity, capacity)],
        )

    own = pl.ds(g * capacity, capacity)
    fetches = [exchange_copy(0, d) for d in rising]
    for copy in fetches:
        copy.start()
    recv_a[own] = send_a[own]

    lax.fori_loop(1, rows_ref.shape[1] // CHUNK, step, 0)

    rims = [[], []]
    grads = []
    for channel in (1, 0):
        for side in range(2):
            rim_ref[0, channel, :, lanes[side]] = acc_ref[channel, side, HALO + band :].astype(half)
            rim_ref[1, channel, :, lanes[side]] = acc_ref[channel, side, :HALO].astype(half)
        for way in range(2):
            where = {"tile": below if way == 0 else upper}
            across = dict(where, half=1 - h)
            index = 6 + way * 5 + channel * 2
            pair_of = [
                near(index, rim_ref.at[way, channel, away, :], rim_here_ref.at[way, h, channel], across),
                near(index + 1, rim_ref.at[way, channel, here, :], rim_here_ref.at[way, h, channel], where),
            ]
            rims[way].append(pair_of)

            def send(copies=pair_of):
                for copy in copies:
                    copy.start()

            when_sent(way, send)
        for side in range(2):
            grad_ref[channel, :, lanes[side]] = acc_ref[channel, side, HALO : HALO + band]
        grads.append(
            near(4 + channel, grad_ref.at[channel, away, :], both_grad_ref.at[h, channel], {"half": 1 - h})
        )
        grads[-1].start()
    for way in range(2):
        where = {"tile": below if way == 0 else upper}
        rims[way].append([near(10 + way * 5, rim_ref.at[way, :, away, :], rim_away_ref.at[way], where)])
        when_sent(way, rims[way][-1][0].start)
    both_grad_ref[h] = grad_ref[:, here, :]

    for copy in fetches:
        copy.wait_recv()
    loads[15].wait()

    def projected(phase, pair):
        total = jnp.zeros((part, RB), jnp.float32)
        for c in range(per_block):
            slot = pair * per_block + c
            picked = recvs[phase][place_ref[slot]]
            total = total + live_ref[slot] * lax.dot_general(
                picked, weight_ref[slot], (((1,), (1,)), ((), ())),
                preferred_element_type=jnp.float32,
            )
        return total

    sinos = [projected(0, pair) for pair in range(pairs)]

    def received(stage):
        for way in range(2):
            def take(copies=rims[way][stage]):
                for copy in copies:
                    copy.wait_recv()

            when_received(way, take)

    def renewed(angle, channel):
        around = both_grad_ref[angle, channel] + rim_here_ref[0, angle, channel].astype(jnp.float32)
        around = around + rim_here_ref[1, angle, channel].astype(jnp.float32)
        return both_base_ref[angle, channel] - descent * around

    base_copy.wait_recv()
    mult_copy.wait_recv()
    grads[0].wait_recv()
    received(0)
    news = [renewed(angle, 1) for angle in range(angles)]
    for pair in range(pairs):
        angle, k = divmod(pair, NRB)
        rays = slice(k * RB, (k + 1) * RB)
        target = news[angle][:, rays] + both_mult_ref[angle, 1, :, rays] / penalty
        residual_ref[pair] = (sinos[pair] - target).astype(half)

    def spread(n):
        slot = slot_ref[n]
        term = dot(residual_ref[lax.div(slot, per_block)], weight_ref[slot])
        return (used_ref[n] * term).astype(half)

    terms = []
    for d in paired:
        peer = lax.rem(g + d, groups)
        for r in range(capacity):
            send_b[peer * capacity + r] = spread(peer * capacity + r)
        terms.append(exchange_copy(1, d))
        terms[-1].start()
    for r in range(capacity):
        recv_b[g * capacity + r] = spread(g * capacity + r)

    width = places * part
    per_tile = LANES // part
    tile_lane = lax.broadcasted_iota(jnp.int32, (1, LANES), 1)
    keys = []
    for first in range(0, places, per_tile):
        key = jnp.zeros((1, LANES), jnp.int32)
        for n in range(first, first + per_tile):
            q, r = divmod(n, capacity)
            key = jnp.where(tile_lane // part == n - first, all_ref[q, r : r + 1, :], key)
        keys.append(key * part + tile_lane % part)
    key = jnp.concatenate(keys, axis=1)
    merge_ref[...] = jnp.where(
        lax.broadcasted_iota(jnp.int32, (reach, width), 0) == key, 1.0, 0.0
    ).astype(half)

    grads[1].wait_recv()
    received(1)
    received(2)
    for angle in range(angles):
        new_mult_ref[angle, 0] = both_mult_ref[angle, 0] + penalty * (renewed(angle, 0) - 1.0)
    for channel in range(2):
        updated_ref[0, channel, here, :] = renewed(h, channel)
        far = grad_ref[channel, away, :] + rim_away_ref[0, channel].astype(jnp.float32)
        far = far + rim_away_ref[1, channel].astype(jnp.float32)
        updated_ref[0, channel, away, :] = base_ref[channel, away, :] - descent * far
    id_local.wait()
    for copy in terms:
        copy.wait_recv()
    total = dot(merge_ref[...], recv_b[...].reshape(width, PIX)).reshape(own_blocks, part, PIX)
    block = vol_ref[...]
    new_vol = block - volume_step * (total + damping * block)
    new_vol_ref[...] = new_vol
    vol_half_ref[...] = new_vol.astype(half)
    renewals = []
    for d in paired:
        peer = lax.rem(g + d, groups)
        for r in range(capacity):
            send_c[peer * capacity + r] = vol_half_ref[all_smem[peer, r, 0]]
        renewals.append(exchange_copy(2, d))
        renewals[-1].start()
    for r in range(capacity):
        recv_c[g * capacity + r] = vol_half_ref[all_smem[g, r, 0]]
    for copy in renewals:
        copy.wait_recv()
    for pair in range(pairs):
        angle, k = divmod(pair, NRB)
        rays = slice(k * RB, (k + 1) * RB)
        fresh = projected(2, pair)
        new_mult_ref[angle, 1, :, rays] = both_mult_ref[angle, 1, :, rays] + penalty * (
            news[angle][:, rays] - fresh
        )
    for copy in id_copies + fetches + terms + renewals + grads + [base_copy, mult_copy]:
        copy.wait_send()
    for way in range(2):
        def settle(copies=sum(rims[way], [halo[way]])):
            for copy in copies:
                copy.wait_send()

        when_sent(way, settle)


def admm_step(ray_blocks, counts, rows, cols, own, multiplier, prior, measured, field, mask, volume, weights):
    groups = lax.axis_size("angle")
    tiles = lax.axis_size("tile")
    slots = ray_blocks.size
    capacity = max(2, -(-slots // groups))
    places = groups * capacity
    left_f, right_f = dft_blocks(-1.0)
    left_b, right_b = dft_blocks(1.0)
    left_f, left_b = (split_table(m) for m in (left_f, left_b))
    tables = [left_f, jnp.asarray(right_f, jnp.bfloat16), left_b, jnp.asarray(right_b, jnp.bfloat16)]
    vmem = pl.BlockSpec(memory_space=pltpu.VMEM)
    band = own.shape[2]
    part = band // 2
    assert band == HALO and capacity <= ROWS
    ext_rows = band + 2 * HALO
    own_blocks = volume.shape[0]
    block = volume.shape[1:]
    weights = weights.reshape((slots,) + weights.shape[3:])
    f32 = jnp.float32
    half = jnp.bfloat16
    operands = [
        ray_blocks, counts, rows, cols, own, multiplier, prior, field, mask, *tables,
        measured, volume, weights,
    ]
    spaces = [pltpu.SMEM] * 4 + [pltpu.VMEM] * 12
    return pl.pallas_call(
        functools.partial(step_kernel, groups, tiles, capacity),
        out_shape=(
            jax.ShapeDtypeStruct(own.shape, f32),
            jax.ShapeDtypeStruct(volume.shape, f32),
            jax.ShapeDtypeStruct((2, 2, part, NW), f32),
        ),
        in_specs=[pl.BlockSpec(memory_space=pltpu.HBM)] * 16,
        out_specs=(vmem, vmem, vmem),
        scratch_shapes=[
            *[space(x.shape, x.dtype) for space, x in zip(spaces, operands)],
            pltpu.SMEM((groups, ROWS, LANES), jnp.int32),
            pltpu.SMEM((slots,), jnp.int32),
            pltpu.SMEM((slots,), jnp.int32),
            pltpu.SMEM((places,), jnp.int32),
            pltpu.SMEM((places,), f32),
            pltpu.SMEM((slots,), f32),
            pltpu.VMEM((groups, ROWS, LANES), jnp.int32),
            pltpu.VMEM((groups, ROWS, LANES), jnp.int32),
            pltpu.VMEM((2, HALO, NW), half),
            pltpu.VMEM((2, HALO, NW), half),
            pltpu.VMEM((2, HALO, NW), half),
            pltpu.VMEM((2, NW // PC, ext_rows, PC), f32),
            pltpu.VMEM((2, NW // PC, ext_rows, PC), f32),
            pltpu.VMEM((2, PR, PC), f32),
            pltpu.VMEM((CHUNK, 2, 2 * (ext_rows - PR) + PR, PC), f32),
            pltpu.VMEM((2, band, NW), f32),
            pltpu.VMEM((2, band, NW), f32),
            *[pltpu.VMEM((2, 2, part, NW), f32)] * 3,
            pltpu.VMEM((2, 2, HALO, NW), half),
            pltpu.VMEM((2, 2, 2, part, NW), half),
            pltpu.VMEM((2, 2, part, NW), half),
            pltpu.VMEM((own_blocks,) + block, half),
            pltpu.VMEM((own_blocks * part, places * part), half),
            pltpu.VMEM((slots // weights_per_block(ray_blocks), part, RB), half),
            *[pltpu.VMEM((places,) + block, half)] * 6,
            pltpu.SemaphoreType.DMA((4, groups)),
            pltpu.SemaphoreType.DMA((4, groups)),
            pltpu.SemaphoreType.DMA((16,)),
            pltpu.SemaphoreType.DMA((16,)),
            pltpu.SemaphoreType.DMA((17,)),
        ],
        compiler_params=pltpu.CompilerParams(
            collective_id=1, has_side_effects=True, vmem_limit_bytes=32 * 1024 * 1024
        ),
    )(*operands)


def weights_per_block(ray_blocks):
    return ray_blocks.shape[2]


def write_kernel(a_ref, b_ref, c_ref, a_out, b_out, c_out, sems):
    copies = [
        pltpu.make_async_copy(source, target, sems.at[i])
        for i, (source, target) in enumerate(((a_ref, a_out), (b_ref, b_out), (c_ref, c_out)))
    ]
    for copy in copies:
        copy.start()
    for copy in copies:
        copy.wait()


def write_out(values):
    return pl.pallas_call(
        write_kernel,
        out_shape=tuple(jax.ShapeDtypeStruct(v.shape, v.dtype) for v in values),
        in_specs=[pl.BlockSpec(memory_space=pltpu.VMEM)] * 3,
        out_specs=tuple([pl.BlockSpec(memory_space=pl.ANY)] * 3),
        scratch_shapes=[pltpu.SemaphoreType.DMA((3,))],
    )(*values)


def shards(
    projection,
    multiplier,
    reprojection,
    intensity,
    row_start,
    column_start,
    probe_field,
    probe_mask,
    weights,
    ray_blocks,
    ray_counts,
    volume,
):
    return write_out(
        admm_step(
            ray_blocks, ray_counts, row_start, column_start, projection, multiplier, reprojection,
            intensity, probe_field, probe_mask, volume, weights,
        )
    )


def solution(mesh):
    return jax.shard_map(
        shards,
        mesh=mesh,
        in_specs=(
            P(("angle", "half"), None, "tile", None),
            P(("angle", "half"), None, "tile", None),
            P(("angle", "half"), "tile", None),
            P(("angle", "half"), "tile", None, None),
            P(("angle", "half"), "tile"),
            P(("angle", "half"), "tile"),
            P(),
            P(),
            P("angle", None, None, None, None),
            P("angle", None, None),
            P("angle", None),
            P("angle", ("tile", "half"), None),
        ),
        out_specs=(
            P(("angle", "half"), None, "tile", None),
            P("angle", ("tile", "half"), None),
            P("angle", None, ("tile", "half"), None),
        ),
        check_vma=False,
    )
```

time: 40.3 us -> 51.4 us (1.28); the launches traced: 40.1 us -> 50.7 us
  local copies, waits for them, and re-layouts: 0 us -> 15.9 us
  Pallas kernels: 39.5 us -> 34.1 us
    unnamed x0 -> x38, local copies, waits for them, and re-layouts: none -> 15.9 us
    pallas_call x1, Pallas kernels: 37.6 us -> 32.2 us  [admm_step(): pl.pallas_call(functools.partial(step_kernel, groups, tiles, capacity), o...]
where the time goes in v1:
time: 51.4 us; the launch traced here: 50.7 us
  Pallas kernels  34.1 us (66%)
  local copies, waits for them, and re-layouts  15.9 us (31%)
  between operations  0.68 us (1%)
    pallas_call x1, Pallas kernels, admm_step(): pl.pallas_call(functools.partial(step_kernel, groups, tiles, capacity), o...  32.2 us
    unnamed x38, local copies, waits for them, and re-layouts  15.9 us
    pallas_call x1, Pallas kernels, write_out(): pl.pallas_call(write_kernel, out_shape=tuple((jax.ShapeDtypeStruct(v.shap...  1.89 us

profile of v1, /device:TPU:0, one launch (start us, length us, event | category | flops | bytes accessed | tf_op | source)
XLA Modules:
  0.0 50.7 jit_solution(10089249157909325594)
XLA Ops:
  0.6 0.0 copy-start
  0.6 1.6 %copy-done = bf16[2,2,4,128,512]{4,3,2,1,0:T(8,128)(2,1)S(1)} copy-done((bf16[2,2,4,128,512]{4,3,2,1,0:T(8,128)(2,1)S(1)}, bf16[2,2,4,128,512]{4,3,2,1,0:T(8,128)(2,1)}, u32[]{:S(2)}) %copy-start) | copy-done | bytes 2097176
  2.2 0.0 copy-start.2
  2.2 1.0 %copy-done.2 = bf16[1,32,64,128]{3,2,1,0:T(8,128)(2,1)S(1)} copy-done((bf16[1,32,64,128]{3,2,1,0:T(8,128)(2,1)S(1)}, bf16[1,32,64,128]{3,2,1,0:T(8,128)(2,1)}, u32[]{:S(2)}) %copy-start.2) | copy-done | bytes 524312
  3.3 0.0 copy-start.3
  3.3 1.0 %copy-done.3 = f32[16,16,512]{2,1,0:T(8,128)S(1)} copy-done((f32[16,16,512]{2,1,0:T(8,128)S(1)}, f32[16,16,512]{2,1,0:T(8,128)}, u32[]{:S(2)}) %copy-start.3) | copy-done | bytes 524312
  4.3 0.0 copy-start.4
  4.3 0.9 %copy-done.4 = bf16[256,256]{1,0:T(8,128)(2,1)S(1)} copy-done((bf16[256,256]{1,0:T(8,128)(2,1)S(1)}, bf16[256,256]{1,0:T(8,128)(2,1)}, u32[]{:S(2)}) %copy-start.4) | copy-done | bytes 131096
  5.2 0.0 copy-start.5
  5.2 0.9 %copy-done.5 = bf16[256,256]{1,0:T(8,128)(2,1)S(1)} copy-done((bf16[256,256]{1,0:T(8,128)(2,1)S(1)}, bf16[256,256]{1,0:T(8,128)(2,1)}, u32[]{:S(2)}) %copy-start.5) | copy-done | bytes 131096
  6.1 0.0 copy-start.6
  6.1 0.8 %copy-done.6 = f32[1,2,32,256]{3,2,1,0:T(8,128)S(1)} copy-done((f32[1,2,32,256]{3,2,1,0:T(8,128)S(1)}, f32[1,2,32,256]{3,2,1,0:T(8,128)}, u32[]{:S(2)}) %copy-start.6) | copy-done | bytes 65560
  7.0 0.0 copy-start.7
  7.0 0.8 %copy-done.7 = f32[1,2,32,256]{3,2,1,0:T(8,128)S(1)} copy-done((f32[1,2,32,256]{3,2,1,0:T(8,128)S(1)}, f32[1,2,32,256]{3,2,1,0:T(8,128)}, u32[]{:S(2)}) %copy-start.7) | copy-done | bytes 65560
  7.8 0.0 copy-start.8
  7.8 0.8 %copy-done.8 = f32[2,64,128]{2,1,0:T(8,128)S(1)} copy-done((f32[2,64,128]{2,1,0:T(8,128)S(1)}, f32[2,64,128]{2,1,0:T(8,128)}, u32[]{:S(2)}) %copy-start.8) | copy-done | bytes 65560
  8.6 0.0 copy-start.9
  8.6 0.8 %copy-done.9 = bf16[128,256]{1,0:T(8,128)(2,1)S(1)} copy-done((bf16[128,256]{1,0:T(8,128)(2,1)S(1)}, bf16[128,256]{1,0:T(8,128)(2,1)}, u32[]{:S(2)}) %copy-start.9) | copy-done | bytes 65560
  9.5 0.0 copy-start.10
  9.5 0.8 %copy-done.10 = bf16[128,256]{1,0:T(8,128)(2,1)S(1)} copy-done((bf16[128,256]{1,0:T(8,128)(2,1)S(1)}, bf16[128,256]{1,0:T(8,128)(2,1)}, u32[]{:S(2)}) %copy-start.10) | copy-done | bytes 65560
  10.3 0.0 copy-start.13
  10.3 0.8 %copy-done.13 = f32[1,32,256]{2,1,0:T(8,128)S(1)} copy-done((f32[1,32,256]{2,1,0:T(8,128)S(1)}, f32[1,32,256]{2,1,0:T(8,128)}, u32[]{:S(2)}) %copy-start.13) | copy-done | bytes 32792
  11.1 0.0 copy-start.14
  11.1 0.8 %copy-done.14 = s32[64,128]{1,0:T(8,128)S(1)} copy-done((s32[64,128]{1,0:T(8,128)S(1)}, s32[64,128]{1,0:T(8,128)}, u32[]{:S(2)}) %copy-start.14) | copy-done | bytes 32792
  11.8 0.0 copy-start.15
  11.8 0.7 %copy-done.15 = s32[2,2,4]{2,1,0:T(2,128)S(1)} copy-done((s32[2,2,4]{2,1,0:T(2,128)S(1)}, s32[2,2,4]{2,1,0:T(2,128)}, u32[]{:S(2)}) %copy-start.15) | copy-done | bytes 88
  12.5 0.0 copy-start.16
  12.5 0.7 %copy-done.16 = s32[2,2]{1,0:T(2,128)S(1)} copy-done((s32[2,2]{1,0:T(2,128)S(1)}, s32[2,2]{1,0:T(2,128)}, u32[]{:S(2)}) %copy-start.16) | copy-done | bytes 40
  13.2 0.0 copy-start.17
  13.2 0.7 %copy-done.17 = s32[1,32]{1,0:T(1,128)S(1)} copy-done((s32[1,32]{1,0:T(1,128)S(1)}, s32[1,32]{1,0:T(1,128)}, u32[]{:S(2)}) %copy-start.17) | copy-done | bytes 152
  13.9 0.0 copy-start.18
  13.9 0.7 %copy-done.18 = s32[1,32]{1,0:T(1,128)S(1)} copy-done((s32[1,32]{1,0:T(1,128)S(1)}, s32[1,32]{1,0:T(1,128)}, u32[]{:S(2)}) %copy-start.18) | copy-done | bytes 152
  14.5 32.2 %shard_map.175 = (f32[1,2,32,256]{3,2,1,0:T(8,128)S(1)}, f32[16,16,512]{2,1,0:T(8,128)S(1)}, f32[2,2,16,256]{3,2,1,0:T(8,128)S(1)}) custom-call(s32[2,2,4]{2,1,0:T(2,128)S(1)} %copy-done.15, s32[2,2]{1,0:T(2,128)S(1)} %copy-done.16, s32[1,32]{1,0:T(1,128)S(1)} %copy-done.17, s32[1,32]{1,0:T(1,128)S(1)} %copy-done.18, f32[1,2,32,256]{3,2,1,0:T(8,128)S(1)} %copy-done.6, ...), custom_call_target="tpu_custom_call" | custom-call | tf_op jit(solution)/shard_map/pallas_call | solution.py:542
  46.8 0.0 copy-start.1
  46.8 0.8 %copy-done.1 = f32[16,16,512]{2,1,0:T(8,128)} copy-done((f32[16,16,512]{2,1,0:T(8,128)}, f32[16,16,512]{2,1,0:T(8,128)S(1)}, u32[]{:S(2)}) %copy-start.1) | copy-done | bytes 524312
  47.6 0.0 copy-start.11
  47.6 0.6 %copy-done.11 = f32[1,2,32,256]{3,2,1,0:T(8,128)} copy-done((f32[1,2,32,256]{3,2,1,0:T(8,128)}, f32[1,2,32,256]{3,2,1,0:T(8,128)S(1)}, u32[]{:S(2)}) %copy-start.11) | copy-done | bytes 65560
  48.2 0.0 copy-start.12
  48.2 0.6 %copy-done.12 = f32[2,2,16,256]{3,2,1,0:T(8,128)} copy-done((f32[2,2,16,256]{3,2,1,0:T(8,128)}, f32[2,2,16,256]{3,2,1,0:T(8,128)S(1)}, u32[]{:S(2)}) %copy-start.12) | copy-done | bytes 65560
  48.8 1.9 %shard_map.176 = (f32[1,2,32,256]{3,2,1,0:T(8,128)}, f32[16,16,512]{2,1,0:T(8,128)}, f32[2,2,16,256]{3,2,1,0:T(8,128)}) custom-call(f32[1,2,32,256]{3,2,1,0:T(8,128)} %copy-done.11, f32[16,16,512]{2,1,0:T(8,128)} %copy-done.1, f32[2,2,16,256]{3,2,1,0:T(8,128)} %copy-done.12), custom_call_target="tpu_custom_call" | custom-call | tf_op jit(solution)/shard_map/pallas_call | solution.py:606
Async XLA Ops:
  0.6 1.6 %copy-start = (bf16[2,2,4,128,512]{4,3,2,1,0:T(8,128)(2,1)S(1)}, bf16[2,2,4,128,512]{4,3,2,1,0:T(8,128)(2,1)}, u32[]{:S(2)}) copy-start(bf16[2,2,4,128,512]{4,3,2,1,0:T(8,128)(2,1)} %param.24) | copy-start | bytes 6291460
  2.2 1.0 %copy-start.2 = (bf16[1,32,64,128]{3,2,1,0:T(8,128)(2,1)S(1)}, bf16[1,32,64,128]{3,2,1,0:T(8,128)(2,1)}, u32[]{:S(2)}) copy-start(bf16[1,32,64,128]{3,2,1,0:T(8,128)(2,1)} %measured_hbm.1) | copy-start | bytes 1572868
  3.3 1.0 %copy-start.3 = (f32[16,16,512]{2,1,0:T(8,128)S(1)}, f32[16,16,512]{2,1,0:T(8,128)}, u32[]{:S(2)}) copy-start(f32[16,16,512]{2,1,0:T(8,128)} %vol_hbm.1) | copy-start | bytes 1572868
  4.3 0.9 %copy-start.4 = (bf16[256,256]{1,0:T(8,128)(2,1)S(1)}, bf16[256,256]{1,0:T(8,128)(2,1)}, u32[]{:S(2)}) copy-start(bf16[256,256]{1,0:T(8,128)(2,1)} %constant.11.clone.right_b_hbm) | copy-start | bytes 393220
  5.2 0.9 %copy-start.5 = (bf16[256,256]{1,0:T(8,128)(2,1)S(1)}, bf16[256,256]{1,0:T(8,128)(2,1)}, u32[]{:S(2)}) copy-start(bf16[256,256]{1,0:T(8,128)(2,1)} %constant.10.clone.right_f_hbm) | copy-start | bytes 393220
  6.1 0.8 %copy-start.6 = (f32[1,2,32,256]{3,2,1,0:T(8,128)S(1)}, f32[1,2,32,256]{3,2,1,0:T(8,128)}, u32[]{:S(2)}) copy-start(f32[1,2,32,256]{3,2,1,0:T(8,128)} %proj_hbm.1) | copy-start | bytes 196612
  7.0 0.8 %copy-start.7 = (f32[1,2,32,256]{3,2,1,0:T(8,128)S(1)}, f32[1,2,32,256]{3,2,1,0:T(8,128)}, u32[]{:S(2)}) copy-start(f32[1,2,32,256]{3,2,1,0:T(8,128)} %mult_hbm.1) | copy-start | bytes 196612
  7.8 0.8 %copy-start.8 = (f32[2,64,128]{2,1,0:T(8,128)S(1)}, f32[2,64,128]{2,1,0:T(8,128)}, u32[]{:S(2)}) copy-start(f32[2,64,128]{2,1,0:T(8,128)} %field_hbm.1) | copy-start | bytes 196612
  8.6 0.8 %copy-start.9 = (bf16[128,256]{1,0:T(8,128)(2,1)S(1)}, bf16[128,256]{1,0:T(8,128)(2,1)}, u32[]{:S(2)}) copy-start(bf16[128,256]{1,0:T(8,128)(2,1)} %constant.9.clone.left_b_hbm) | copy-start | bytes 196612
  9.5 0.8 %copy-start.10 = (bf16[128,256]{1,0:T(8,128)(2,1)S(1)}, bf16[128,256]{1,0:T(8,128)(2,1)}, u32[]{:S(2)}) copy-start(bf16[128,256]{1,0:T(8,128)(2,1)} %constant.8.clone.left_f_hbm) | copy-start | bytes 196612
  10.3 0.8 %copy-start.13 = (f32[1,32,256]{2,1,0:T(8,128)S(1)}, f32[1,32,256]{2,1,0:T(8,128)}, u32[]{:S(2)}) copy-start(f32[1,32,256]{2,1,0:T(8,128)} %prior_hbm.1) | copy-start | bytes 98308
  11.1 0.8 %copy-start.14 = (s32[64,128]{1,0:T(8,128)S(1)}, s32[64,128]{1,0:T(8,128)}, u32[]{:S(2)}) copy-start(s32[64,128]{1,0:T(8,128)} %mask_hbm.1) | copy-start | bytes 98308
  11.8 0.7 %copy-start.15 = (s32[2,2,4]{2,1,0:T(2,128)S(1)}, s32[2,2,4]{2,1,0:T(2,128)}, u32[]{:S(2)}) copy-start(s32[2,2,4]{2,1,0:T(2,128)} %mine_hbm.1) | copy-start | bytes 196
  12.5 0.7 %copy-start.16 = (s32[2,2]{1,0:T(2,128)S(1)}, s32[2,2]{1,0:T(2,128)}, u32[]{:S(2)}) copy-start(s32[2,2]{1,0:T(2,128)} %counts_hbm.1) | copy-start | bytes 52
  13.2 0.7 %copy-start.17 = (s32[1,32]{1,0:T(1,128)S(1)}, s32[1,32]{1,0:T(1,128)}, u32[]{:S(2)}) copy-start(s32[1,32]{1,0:T(1,128)} %rows_hbm.1) | copy-start | bytes 388
  13.9 0.7 %copy-start.18 = (s32[1,32]{1,0:T(1,128)S(1)}, s32[1,32]{1,0:T(1,128)}, u32[]{:S(2)}) copy-start(s32[1,32]{1,0:T(1,128)} %cols_hbm.1) | copy-start | bytes 388
  46.8 0.8 %copy-start.1 = (f32[16,16,512]{2,1,0:T(8,128)}, f32[16,16,512]{2,1,0:T(8,128)S(1)}, u32[]{:S(2)}) copy-start(f32[16,16,512]{2,1,0:T(8,128)S(1)} %get-tuple-element.7.b_ref) | copy-start | bytes 1572868
  47.6 0.6 %copy-start.11 = (f32[1,2,32,256]{3,2,1,0:T(8,128)}, f32[1,2,32,256]{3,2,1,0:T(8,128)S(1)}, u32[]{:S(2)}) copy-start(f32[1,2,32,256]{3,2,1,0:T(8,128)S(1)} %get-tuple-element.6.a_ref) | copy-start | bytes 196612
  48.2 0.6 %copy-start.12 = (f32[2,2,16,256]{3,2,1,0:T(8,128)}, f32[2,2,16,256]{3,2,1,0:T(8,128)S(1)}, u32[]{:S(2)}) copy-start(f32[2,2,16,256]{3,2,1,0:T(8,128)S(1)} %get-tuple-element.8.c_ref) | copy-start | bytes 196612

commit v2 on v1

--- a/solution.py
+++ b/solution.py
@@ -584,7 +584,7 @@
         compiler_params=pltpu.CompilerParams(
             collective_id=1, has_side_effects=True, vmem_limit_bytes=32 * 1024 * 1024
         ),
-    )(*operands)
+    )(*[pltpu.with_memory_space_constraint(x, pltpu.HBM) for x in operands])
 
 
 def weights_per_block(ray_blocks):
@@ -609,6 +609,7 @@
         in_specs=[pl.BlockSpec(memory_space=pltpu.VMEM)] * 3,
         out_specs=tuple([pl.BlockSpec(memory_space=pl.ANY)] * 3),
         scratch_shapes=[pltpu.SemaphoreType.DMA((3,))],
+        compiler_params=pltpu.CompilerParams(vmem_limit_bytes=8 * 1024 * 1024),
     )(*values)
 
 

time: 51.4 us -> 35.3 us (0.69); the launches traced: 50.7 us -> 35.2 us
  local copies, waits for them, and re-layouts: 15.9 us -> 0 us
    unnamed x38 -> x0, local copies, waits for them, and re-layouts: 15.9 us -> none
    pallas_call x1, Pallas kernels: 32.2 us -> 33.7 us  [admm_step(): pl.pallas_call(functools.partial(step_kernel, groups, tiles, capacity), o...]
    pallas_call x1, Pallas kernels: 1.89 us -> 0.85 us  [write_out(): pl.pallas_call(write_kernel, out_shape=tuple((jax.ShapeDtypeStruct(v.shap...]
where the time goes in v2:
time: 35.3 us; the launch traced here: 35.2 us
  Pallas kernels  34.5 us (98%)
  between operations  0.64 us (2%)
    pallas_call x1, Pallas kernels, admm_step(): pl.pallas_call(functools.partial(step_kernel, groups, tiles, capacity), o...  33.7 us
    pallas_call x1, Pallas kernels, write_out(): pl.pallas_call(write_kernel, out_shape=tuple((jax.ShapeDtypeStruct(v.shap...  0.85 us

profile of v2, /device:TPU:0, one launch (start us, length us, event | category | flops | bytes accessed | tf_op | source)
XLA Modules:
  0.0 35.2 jit_solution(5117514893416678142)
XLA Ops:
  0.6 33.7 %shard_map.175 = (f32[1,2,32,256]{3,2,1,0:T(8,128)S(1)}, f32[16,16,512]{2,1,0:T(8,128)S(1)}, f32[2,2,16,256]{3,2,1,0:T(8,128)S(1)}) custom-call(s32[2,2,4]{2,1,0:T(2,128)} %mine_hbm.1, s32[2,2]{1,0:T(2,128)} %counts_hbm.1, s32[1,32]{1,0:T(1,128)} %rows_hbm.1, s32[1,32]{1,0:T(1,128)} %cols_hbm.1, f32[1,2,32,256]{3,2,1,0:T(8,128)} %proj_hbm.1, ...), custom_call_target="tpu_custom_call" | custom-call | tf_op jit(solution)/shard_map/pallas_call | solution.py:542
  34.3 0.9 %shard_map.176 = (f32[1,2,32,256]{3,2,1,0:T(8,128)}, f32[16,16,512]{2,1,0:T(8,128)}, f32[2,2,16,256]{3,2,1,0:T(8,128)}) custom-call(f32[1,2,32,256]{3,2,1,0:T(8,128)S(1)} %get-tuple-element.6.a_ref, f32[16,16,512]{2,1,0:T(8,128)S(1)} %get-tuple-element.7.b_ref, f32[2,2,16,256]{3,2,1,0:T(8,128)S(1)} %get-tuple-element.8.c_ref), custom_call_target="tpu_custom_call" | custom-call | tf_op jit(solution)/shard_map/pallas_call | solution.py:606

commit v3 on v2

--- a/solution.py
+++ b/solution.py
@@ -51,12 +51,16 @@
 
 def orders(groups):
     rising = list(range(1, groups))
-    paired = []
-    for d in range(1, groups // 2 + 1):
-        paired += [groups - d] if 2 * d == groups else [groups - d, d]
-    if groups % 2:
-        paired = rising
-    return rising, paired
+    return rising, [groups // 2] + [d for d in reversed(rising) if 2 * d != groups]
+
+
+def flipped(index, mask, count):
+    out = jnp.int32(0)
+    bit = 1
+    while bit < count:
+        out = out + lax.rem(lax.div(index, bit) + mask // bit, 2) * bit
+        bit *= 2
+    return out
 
 
 def step_kernel(
@@ -72,6 +76,7 @@
     base_ref, grad_ref, both_base_ref, both_mult_ref, both_grad_ref,
     rim_ref, rim_here_ref, rim_away_ref,
     vol_half_ref, merge_ref, residual_ref,
+    tile_ref, far_tile_ref, twin_send_ref, twin_recv_ref, part_send_ref, part_recv_ref,
     send_a, send_b, send_c, recv_a, recv_b, recv_c,
     send_sem, recv_sem, near_send, near_recv, local_sem,
 ):
@@ -92,6 +97,11 @@
     recvs = (recv_a, recv_b, recv_c)
     lanes = [slice(0, PC), slice(PC, NW)]
     rising, paired = orders(groups)
+    peers = {m: flipped(g, m, groups) for m in rising}
+    across = groups // 2
+    twin = lax.rem(g + across, groups)
+    column = lax.rem(t, 2)
+    quarter = RB // 4
 
     def where_of(slot):
         pair, c = divmod(slot, per_block)
@@ -104,7 +114,7 @@
         pl.semaphore_signal(barrier, inc=1, device_id=where, device_id_type=MESH)
 
     for d in rising:
-        greet({"angle": lax.rem(g + d, groups)})
+        greet({"angle": peers[d]})
     greet({"half": 1 - h})
 
     @pl.when(has_up)
@@ -195,6 +205,11 @@
     both_mult_ref[h] = mult_ref[0, :, here, :]
     loads[14].wait()
     vol_half_ref[...] = vol_ref[...].astype(half)
+    loads[15].wait()
+    first_ray = pl.multiple_of((2 * h + column) * quarter, quarter)
+    for r in range(capacity):
+        tile_ref[r] = weight_ref[slot_ref[twin * capacity + r], pl.ds(first_ray, quarter), :]
+        recv_c[twin * capacity + r] = jnp.zeros(recv_c.shape[1:], half)
 
     pl.semaphore_wait(
         barrier, groups + 2 * has_up.astype(jnp.int32) + 2 * has_down.astype(jnp.int32)
@@ -206,7 +221,7 @@
             dst_ref=target,
             send_sem=send_sem.at[phase, d],
             recv_sem=recv_sem.at[phase, d],
-            device_id={"angle": lax.rem(g + d, groups)},
+            device_id={"angle": peers[d]},
             device_id_type=MESH,
         )
 
@@ -230,10 +245,12 @@
         pl.when(has_up if way == 0 else has_down)(act)
 
     id_copies = [
-        angle_copy(3, d, ids_ref.at[lax.rem(g + d, groups)], all_ref.at[g]) for d in rising
+        angle_copy(3, d, ids_ref.at[peers[d]], all_ref.at[g]) for d in rising
     ]
     for copy in id_copies:
         copy.start()
+    tile_copy = angle_copy(4, across, tile_ref, far_tile_ref.at[h, column])
+    tile_copy.start()
     halo = [
         near(0, edge_ref, before_ref, {"tile": below}),
         near(1, edge_ref, after_ref, {"tile": upper}),
@@ -349,7 +366,7 @@
         send_a[n] = gathered[n * part : (n + 1) * part]
 
     def exchange_copy(phase, d):
-        peer = lax.rem(g + d, groups)
+        peer = peers[d]
         return angle_copy(
             phase, d,
             sends[phase].at[pl.ds(peer * capacity, capacity)],
@@ -372,10 +389,10 @@
             rim_ref[1, channel, :, lanes[side]] = acc_ref[channel, side, :HALO].astype(half)
         for way in range(2):
             where = {"tile": below if way == 0 else upper}
-            across = dict(where, half=1 - h)
+            other = dict(where, half=1 - h)
             index = 6 + way * 5 + channel * 2
             pair_of = [
-                near(index, rim_ref.at[way, channel, away, :], rim_here_ref.at[way, h, channel], across),
+                near(index, rim_ref.at[way, channel, away, :], rim_here_ref.at[way, h, channel], other),
                 near(index + 1, rim_ref.at[way, channel, here, :], rim_here_ref.at[way, h, channel], where),
             ]
             rims[way].append(pair_of)
@@ -396,10 +413,12 @@
         rims[way].append([near(10 + way * 5, rim_ref.at[way, :, away, :], rim_away_ref.at[way], where)])
         when_sent(way, rims[way][-1][0].start)
     both_grad_ref[h] = grad_ref[:, here, :]
+    tile_copy.wait_recv()
+    beside = near(16, far_tile_ref.at[h, column], far_tile_ref.at[h, column], {"tile": t + 1 - 2 * column})
+    beside.start()
 
     for copy in fetches:
         copy.wait_recv()
-    loads[15].wait()
 
     def projected(phase, pair):
         total = jnp.zeros((part, RB), jnp.float32)
@@ -443,15 +462,25 @@
         term = dot(residual_ref[lax.div(slot, per_block)], weight_ref[slot])
         return (used_ref[n] * term).astype(half)
 
-    terms = []
+    for r in range(capacity):
+        n = twin * capacity + r
+        twin_send_ref[r] = residual_ref[lax.div(slot_ref[n], per_block)] * used_ref[n].astype(half)
+    terms = [angle_copy(1, across, twin_send_ref, twin_recv_ref)]
+    terms[0].start()
     for d in paired:
-        peer = lax.rem(g + d, groups)
+        if d == across:
+            continue
+        peer = peers[d]
         for r in range(capacity):
             send_b[peer * capacity + r] = spread(peer * capacity + r)
         terms.append(exchange_copy(1, d))
         terms[-1].start()
     for r in range(capacity):
         recv_b[g * capacity + r] = spread(g * capacity + r)
+
+    beside.wait_recv()
+    inside = near(17, far_tile_ref.at[h], far_tile_ref.at[h], {"half": 1 - h})
+    inside.start()
 
     width = places * part
     per_tile = LANES // part
@@ -479,16 +508,32 @@
         far = far + rim_away_ref[1, channel].astype(jnp.float32)
         updated_ref[0, channel, away, :] = base_ref[channel, away, :] - descent * far
     id_local.wait()
-    for copy in terms:
+    inside.wait_recv()
+    terms[0].wait_recv()
+    far_tiles = [
+        jnp.concatenate([far_tile_ref[k // 2, k % 2, r] for k in range(4)], axis=0)
+        for r in range(capacity)
+    ]
+    for r in range(capacity):
+        recv_b[twin * capacity + r] = dot(twin_recv_ref[r], far_tiles[r]).astype(half)
+    for copy in terms[1:]:
         copy.wait_recv()
     total = dot(merge_ref[...], recv_b[...].reshape(width, PIX)).reshape(own_blocks, part, PIX)
     block = vol_ref[...]
     new_vol = block - volume_step * (total + damping * block)
     new_vol_ref[...] = new_vol
     vol_half_ref[...] = new_vol.astype(half)
-    renewals = []
+    for r in range(capacity):
+        part_send_ref[r] = lax.dot_general(
+            vol_half_ref[all_smem[twin, r, 0]], far_tiles[r], (((1,), (1,)), ((), ())),
+            preferred_element_type=jnp.float32,
+        ).astype(half)
+    renewals = [angle_copy(2, across, part_send_ref, part_recv_ref)]
+    renewals[0].start()
     for d in paired:
-        peer = lax.rem(g + d, groups)
+        if d == across:
+            continue
+        peer = peers[d]
         for r in range(capacity):
             send_c[peer * capacity + r] = vol_half_ref[all_smem[peer, r, 0]]
         renewals.append(exchange_copy(2, d))
@@ -501,10 +546,14 @@
         angle, k = divmod(pair, NRB)
         rays = slice(k * RB, (k + 1) * RB)
         fresh = projected(2, pair)
+        for r in range(capacity):
+            n = twin * capacity + r
+            mine = jnp.where(lax.div(slot_ref[n], per_block) == pair, used_ref[n], 0.0)
+            fresh = fresh + mine * part_recv_ref[r].astype(jnp.float32)
         new_mult_ref[angle, 1, :, rays] = both_mult_ref[angle, 1, :, rays] + penalty * (
             news[angle][:, rays] - fresh
         )
-    for copy in id_copies + fetches + terms + renewals + grads + [base_copy, mult_copy]:
+    for copy in id_copies + fetches + terms + renewals + grads + [base_copy, mult_copy, tile_copy, beside, inside]:
         copy.wait_send()
     for way in range(2):
         def settle(copies=sum(rims[way], [halo[way]])):
@@ -527,7 +576,7 @@
     vmem = pl.BlockSpec(memory_space=pltpu.VMEM)
     band = own.shape[2]
     part = band // 2
-    assert band == HALO and capacity <= ROWS
+    assert band == HALO and capacity <= ROWS and groups & (groups - 1) == 0 and tiles % 2 == 0
     ext_rows = band + 2 * HALO
     own_blocks = volume.shape[0]
     block = volume.shape[1:]
@@ -574,11 +623,14 @@
             pltpu.VMEM((own_blocks,) + block, half),
             pltpu.VMEM((own_blocks * part, places * part), half),
             pltpu.VMEM((slots // weights_per_block(ray_blocks), part, RB), half),
+            pltpu.VMEM((capacity, RB // 4, PIX), half),
+            pltpu.VMEM((2, 2, capacity, RB // 4, PIX), half),
+            *[pltpu.VMEM((capacity, part, RB), half)] * 4,
             *[pltpu.VMEM((places,) + block, half)] * 6,
-            pltpu.SemaphoreType.DMA((4, groups)),
-            pltpu.SemaphoreType.DMA((4, groups)),
-            pltpu.SemaphoreType.DMA((16,)),
-            pltpu.SemaphoreType.DMA((16,)),
+            pltpu.SemaphoreType.DMA((5, groups)),
+            pltpu.SemaphoreType.DMA((5, groups)),
+            pltpu.SemaphoreType.DMA((18,)),
+            pltpu.SemaphoreType.DMA((18,)),
             pltpu.SemaphoreType.DMA((17,)),
         ],
         compiler_params=pltpu.CompilerParams(

time: 35.3 us -> 33.2 us (0.941)
  Pallas kernels: 34.5 us -> 32.4 us
    pallas_call x1, Pallas kernels: 33.7 us -> 31.6 us  [admm_step(): pl.pallas_call(functools.partial(step_kernel, groups, tiles, capacity), o...]
where the time goes in v3:
time: 33.2 us; the launch traced here: 33.1 us
  Pallas kernels  32.4 us (98%)
  between operations  0.64 us (2%)
    pallas_call x1, Pallas kernels, admm_step(): pl.pallas_call(functools.partial(step_kernel, groups, tiles, capacity), o...  31.6 us
    pallas_call x1, Pallas kernels, write_out(): pl.pallas_call(write_kernel, out_shape=tuple((jax.ShapeDtypeStruct(v.shap...  0.85 us

profile of v3, /device:TPU:0, one launch (start us, length us, event | category | flops | bytes accessed | tf_op | source)
XLA Modules:
  0.0 33.1 jit_solution(17393120342825072524)
XLA Ops:
  0.6 31.6 %shard_map.175 = (f32[1,2,32,256]{3,2,1,0:T(8,128)S(1)}, f32[16,16,512]{2,1,0:T(8,128)S(1)}, f32[2,2,16,256]{3,2,1,0:T(8,128)S(1)}) custom-call(s32[2,2,4]{2,1,0:T(2,128)} %mine_hbm.1, s32[2,2]{1,0:T(2,128)} %counts_hbm.1, s32[1,32]{1,0:T(1,128)} %rows_hbm.1, s32[1,32]{1,0:T(1,128)} %cols_hbm.1, f32[1,2,32,256]{3,2,1,0:T(8,128)} %proj_hbm.1, ...), custom_call_target="tpu_custom_call" | custom-call | tf_op jit(solution)/shard_map/pallas_call | solution.py:591
  32.2 0.9 %shard_map.176 = (f32[1,2,32,256]{3,2,1,0:T(8,128)}, f32[16,16,512]{2,1,0:T(8,128)}, f32[2,2,16,256]{3,2,1,0:T(8,128)}) custom-call(f32[1,2,32,256]{3,2,1,0:T(8,128)S(1)} %get-tuple-element.6.a_ref, f32[16,16,512]{2,1,0:T(8,128)S(1)} %get-tuple-element.7.b_ref, f32[2,2,16,256]{3,2,1,0:T(8,128)S(1)} %get-tuple-element.8.c_ref), custom_call_target="tpu_custom_call" | custom-call | tf_op jit(solution)/shard_map/pallas_call | solution.py:658

commit v4 on v3

--- a/solution.py
+++ b/solution.py
@@ -203,14 +203,6 @@
     wave_ref[1] = field_ref[1] * mask
     both_base_ref[h] = base_ref[:, here, :]
     both_mult_ref[h] = mult_ref[0, :, here, :]
-    loads[14].wait()
-    vol_half_ref[...] = vol_ref[...].astype(half)
-    loads[15].wait()
-    first_ray = pl.multiple_of((2 * h + column) * quarter, quarter)
-    for r in range(capacity):
-        tile_ref[r] = weight_ref[slot_ref[twin * capacity + r], pl.ds(first_ray, quarter), :]
-        recv_c[twin * capacity + r] = jnp.zeros(recv_c.shape[1:], half)
-
     pl.semaphore_wait(
         barrier, groups + 2 * has_up.astype(jnp.int32) + 2 * has_down.astype(jnp.int32)
     )
@@ -249,8 +241,6 @@
     ]
     for copy in id_copies:
         copy.start()
-    tile_copy = angle_copy(4, across, tile_ref, far_tile_ref.at[h, column])
-    tile_copy.start()
     halo = [
         near(0, edge_ref, before_ref, {"tile": below}),
         near(1, edge_ref, after_ref, {"tile": upper}),
@@ -261,6 +251,16 @@
     mult_copy = near(3, mult_ref.at[0, :, away, :], both_mult_ref.at[h], {"half": 1 - h})
     base_copy.start()
     mult_copy.start()
+    loads[14].wait()
+    vol_half_ref[...] = vol_ref[...].astype(half)
+    loads[15].wait()
+    first_ray = pl.multiple_of((2 * h + column) * quarter, quarter)
+    for r in range(capacity):
+        tile_ref[r] = weight_ref[slot_ref[twin * capacity + r], pl.ds(first_ray, quarter), :]
+        recv_c[twin * capacity + r] = jnp.zeros(recv_c.shape[1:], half)
+
+    tile_copy = angle_copy(4, across, tile_ref, far_tile_ref.at[h, column])
+    tile_copy.start()
     all_ref[g] = ids_ref[g]
     for load in loads[2:4] + loads[9:14]:
         load.wait()

time: 33.2 us -> 32.5 us (0.979)
  Pallas kernels: 32.4 us -> 31.7 us
    pallas_call x1, Pallas kernels: 31.6 us -> 30.8 us  [admm_step(): pl.pallas_call(functools.partial(step_kernel, groups, tiles, capacity), o...]
where the time goes in v4:
time: 32.5 us; the launch traced here: 32.3 us
  Pallas kernels  31.7 us (98%)
  between operations  0.64 us (2%)
    pallas_call x1, Pallas kernels, admm_step(): pl.pallas_call(functools.partial(step_kernel, groups, tiles, capacity), o...  30.8 us
    pallas_call x1, Pallas kernels, write_out(): pl.pallas_call(write_kernel, out_shape=tuple((jax.ShapeDtypeStruct(v.shap...  0.85 us

profile of v4, /device:TPU:0, one launch (start us, length us, event | category | flops | bytes accessed | tf_op | source)
XLA Modules:
  0.0 32.3 jit_solution(2662167480698024929)
XLA Ops:
  0.6 30.8 %shard_map.175 = (f32[1,2,32,256]{3,2,1,0:T(8,128)S(1)}, f32[16,16,512]{2,1,0:T(8,128)S(1)}, f32[2,2,16,256]{3,2,1,0:T(8,128)S(1)}) custom-call(s32[2,2,4]{2,1,0:T(2,128)} %mine_hbm.1, s32[2,2]{1,0:T(2,128)} %counts_hbm.1, s32[1,32]{1,0:T(1,128)} %rows_hbm.1, s32[1,32]{1,0:T(1,128)} %cols_hbm.1, f32[1,2,32,256]{3,2,1,0:T(8,128)} %proj_hbm.1, ...), custom_call_target="tpu_custom_call" | custom-call | tf_op jit(solution)/shard_map/pallas_call | solution.py:591
  31.4 0.9 %shard_map.176 = (f32[1,2,32,256]{3,2,1,0:T(8,128)}, f32[16,16,512]{2,1,0:T(8,128)}, f32[2,2,16,256]{3,2,1,0:T(8,128)}) custom-call(f32[1,2,32,256]{3,2,1,0:T(8,128)S(1)} %get-tuple-element.6.a_ref, f32[16,16,512]{2,1,0:T(8,128)S(1)} %get-tuple-element.7.b_ref, f32[2,2,16,256]{3,2,1,0:T(8,128)S(1)} %get-tuple-element.8.c_ref), custom_call_target="tpu_custom_call" | custom-call | tf_op jit(solution)/shard_map/pallas_call | solution.py:658

commit v5 on v4

--- a/solution.py
+++ b/solution.py
@@ -257,7 +257,6 @@
     first_ray = pl.multiple_of((2 * h + column) * quarter, quarter)
     for r in range(capacity):
         tile_ref[r] = weight_ref[slot_ref[twin * capacity + r], pl.ds(first_ray, quarter), :]
-        recv_c[twin * capacity + r] = jnp.zeros(recv_c.shape[1:], half)
 
     tile_copy = angle_copy(4, across, tile_ref, far_tile_ref.at[h, column])
     tile_copy.start()
@@ -417,8 +416,22 @@
     beside = near(16, far_tile_ref.at[h, column], far_tile_ref.at[h, column], {"tile": t + 1 - 2 * column})
     beside.start()
 
-    for copy in fetches:
-        copy.wait_recv()
+    def projections(phase, arrivals):
+        totals = [jnp.zeros((part, RB), jnp.float32)] * pairs
+        for peer, copy in [(g, None)] + arrivals:
+            if copy is not None:
+                copy.wait_recv()
+            for r in range(capacity):
+                n = peer * capacity + r
+                slot = slot_ref[n]
+                term = lax.dot_general(
+                    recvs[phase][n], weight_ref[slot], (((1,), (1,)), ((), ())),
+                    preferred_element_type=jnp.float32,
+                )
+                for pair in range(pairs):
+                    scale = jnp.where(lax.div(slot, per_block) == pair, used_ref[n], 0.0)
+                    totals[pair] = totals[pair] + scale * term
+        return totals
 
     def projected(phase, pair):
         total = jnp.zeros((part, RB), jnp.float32)
@@ -431,6 +444,8 @@
             )
         return total
 
+    for copy in fetches:
+        copy.wait_recv()
     sinos = [projected(0, pair) for pair in range(pairs)]
 
     def received(stage):
@@ -540,12 +555,13 @@
         renewals[-1].start()
     for r in range(capacity):
         recv_c[g * capacity + r] = vol_half_ref[all_smem[g, r, 0]]
-    for copy in renewals:
-        copy.wait_recv()
+    by_mask = dict(zip([d for d in paired if d != across], renewals[1:]))
+    freshes = projections(2, [(peers[d], by_mask[d]) for d in rising if d != across])
+    renewals[0].wait_recv()
     for pair in range(pairs):
         angle, k = divmod(pair, NRB)
         rays = slice(k * RB, (k + 1) * RB)
-        fresh = projected(2, pair)
+        fresh = freshes[pair]
         for r in range(capacity):
             n = twin * capacity + r
             mine = jnp.where(lax.div(slot_ref[n], per_block) == pair, used_ref[n], 0.0)

time: 32.5 us -> 32.2 us (level)
  no operation moved by 1% of the time
where the time goes in v5:
time: 32.2 us; the launch traced here: 32 us
  Pallas kernels  31.4 us (98%)
  between operations  0.64 us (2%)
    pallas_call x1, Pallas kernels, admm_step(): pl.pallas_call(functools.partial(step_kernel, groups, tiles, capacity), o...  30.5 us
    pallas_call x1, Pallas kernels, write_out(): pl.pallas_call(write_kernel, out_shape=tuple((jax.ShapeDtypeStruct(v.shap...  0.85 us

profile of v5, /device:TPU:0, one launch (start us, length us, event | category | flops | bytes accessed | tf_op | source)
XLA Modules:
  0.0 32.0 jit_solution(5809613216738855766)
XLA Ops:
  0.6 30.5 %shard_map.175 = (f32[1,2,32,256]{3,2,1,0:T(8,128)S(1)}, f32[16,16,512]{2,1,0:T(8,128)S(1)}, f32[2,2,16,256]{3,2,1,0:T(8,128)S(1)}) custom-call(s32[2,2,4]{2,1,0:T(2,128)} %mine_hbm.1, s32[2,2]{1,0:T(2,128)} %counts_hbm.1, s32[1,32]{1,0:T(1,128)} %rows_hbm.1, s32[1,32]{1,0:T(1,128)} %cols_hbm.1, f32[1,2,32,256]{3,2,1,0:T(8,128)} %proj_hbm.1, ...), custom_call_target="tpu_custom_call" | custom-call | tf_op jit(solution)/shard_map/pallas_call | solution.py:607
  31.2 0.9 %shard_map.176 = (f32[1,2,32,256]{3,2,1,0:T(8,128)}, f32[16,16,512]{2,1,0:T(8,128)}, f32[2,2,16,256]{3,2,1,0:T(8,128)}) custom-call(f32[1,2,32,256]{3,2,1,0:T(8,128)S(1)} %get-tuple-element.6.a_ref, f32[16,16,512]{2,1,0:T(8,128)S(1)} %get-tuple-element.7.b_ref, f32[2,2,16,256]{3,2,1,0:T(8,128)S(1)} %get-tuple-element.8.c_ref), custom_call_target="tpu_custom_call" | custom-call | tf_op jit(solution)/shard_map/pallas_call | solution.py:674

commit v6 on v5

--- a/solution.py
+++ b/solution.py
@@ -98,8 +98,10 @@
     lanes = [slice(0, PC), slice(PC, NW)]
     rising, paired = orders(groups)
     peers = {m: flipped(g, m, groups) for m in rising}
+    for m in [m for m in rising[1:] if m // 2 != groups // 4]:
+        peers[m] = peers[m] + h * (1 - 2 * lax.rem(peers[m], 2))
     across = groups // 2
-    twin = lax.rem(g + across, groups)
+    twin = peers[across]
     column = lax.rem(t, 2)
     quarter = RB // 4
 

time: 32.2 us -> 32.2 us (level)
  no operation moved by 1% of the time
where the time goes in v6:
time: 32.2 us; the launch traced here: 32 us
  Pallas kernels  31.3 us (97%)
  between operations  0.64 us (2%)
    pallas_call x1, Pallas kernels, admm_step(): pl.pallas_call(functools.partial(step_kernel, groups, tiles, capacity), o...  30.5 us
    pallas_call x1, Pallas kernels, write_out(): pl.pallas_call(write_kernel, out_shape=tuple((jax.ShapeDtypeStruct(v.shap...  0.85 us

profile of v6, /device:TPU:0, one launch (start us, length us, event | category | flops | bytes accessed | tf_op | source)
XLA Modules:
  0.0 32.0 jit_solution(11358805239662004093)
XLA Ops:
  0.6 30.5 %shard_map.175 = (f32[1,2,32,256]{3,2,1,0:T(8,128)S(1)}, f32[16,16,512]{2,1,0:T(8,128)S(1)}, f32[2,2,16,256]{3,2,1,0:T(8,128)S(1)}) custom-call(s32[2,2,4]{2,1,0:T(2,128)} %mine_hbm.1, s32[2,2]{1,0:T(2,128)} %counts_hbm.1, s32[1,32]{1,0:T(1,128)} %rows_hbm.1, s32[1,32]{1,0:T(1,128)} %cols_hbm.1, f32[1,2,32,256]{3,2,1,0:T(8,128)} %proj_hbm.1, ...), custom_call_target="tpu_custom_call" | custom-call | tf_op jit(solution)/shard_map/pallas_call | solution.py:609
  31.1 0.9 %shard_map.176 = (f32[1,2,32,256]{3,2,1,0:T(8,128)}, f32[16,16,512]{2,1,0:T(8,128)}, f32[2,2,16,256]{3,2,1,0:T(8,128)}) custom-call(f32[1,2,32,256]{3,2,1,0:T(8,128)S(1)} %get-tuple-element.6.a_ref, f32[16,16,512]{2,1,0:T(8,128)S(1)} %get-tuple-element.7.b_ref, f32[2,2,16,256]{3,2,1,0:T(8,128)S(1)} %get-tuple-element.8.c_ref), custom_call_target="tpu_custom_call" | custom-call | tf_op jit(solution)/shard_map/pallas_call | solution.py:676
